TPU v7x, 32 devices: a whole 2x2x4 slice. The times are simulated.
32 devices in a mesh: freq: 8 (over z, x), pol: 2 (over core), beam: 2 (over y).
Axes of the slice: x: 2, y: 2, z: 4, core: 2. Of those that a mesh axis runs over, the one named last changes fastest.
Arguments:
- voltages: bfloat16 [1024, 2, 256, 512], P('freq', 'pol', 'beam'), may hold values from -6 to 6
- beam_weights: bfloat16 [256, 2, 1024, 512], P('freq', None, None, 'beam'), may hold values from -0.125 to 0.125
- delay_shifts: int32 [8, 256], replicated, may hold values from 0 to 255, as said below
Outputs:
- dedispersed: float32 [256, 2, 256, 256], P('freq', 'beam', 'pol')
Inputs may be any that keep to these rules, and one draw needn't show every extreme that they name: delay_shifts[s, d] lies between (d + 1) // 2 and d; only entries with d below 2 ** (s + 1) are read.
All inputs are finite; a program needn't handle non-finite values.
Results may differ from a plain program's by a relative error of at most 0.0006.
Values may be sent and summed in bfloat16 or wider, within the bound.
A program may use at most 256 MiB of HBM per device.

v0:
```python
import math
import jax
import jax.numpy as jnp
from jax import lax
from jax.sharding import PartitionSpec as P

F = 256


def swapped(shard, axis, bit):
    return lax.ppermute(shard, axis, [(i, i ^ 1 << bit) for i in range(lax.axis_size(axis))])


def fourier_table(length):
    index_row = jnp.arange(length, dtype=jnp.int32)
    product = index_row[:, None] * index_row[None, :] % length
    phase_angle = 2.0 * math.pi / length * product.astype(jnp.float32)
    norm_scale = 1.0 / math.sqrt(length)
    cosine = jnp.cos(phase_angle) * norm_scale
    sine_part = jnp.sin(phase_angle) * norm_scale
    real_rows = jnp.concatenate([cosine, sine_part], axis=1)
    imag_rows = jnp.concatenate([-sine_part, cosine], axis=1)
    return jnp.concatenate([real_rows, imag_rows], axis=0).astype(jnp.bfloat16)


def shift_rows(planes, amounts):
    length = planes.shape[-1]
    padded = jnp.concatenate([planes, jnp.zeros_like(planes)], axis=-1)
    return jax.vmap(
        lambda single_plane, amount: lax.dynamic_slice_in_dim(single_plane, amount, length, axis=1)
    )(padded, amounts)


def merge_level(planes, shift_row):
    first_half = planes[0::2]
    second_half = planes[1::2]
    widened = 2 * planes.shape[1]
    first_rep = jnp.repeat(first_half, 2, axis=1)
    second_rep = jnp.repeat(second_half, 2, axis=1)
    amounts = shift_row[:widened]
    shifted = jax.vmap(shift_rows, in_axes=(0, None))(second_rep, amounts)
    return first_rep + shifted


def contract(weights_part, volts_part):
    return jnp.einsum("cab,cas->cbs", weights_part, volts_part, preferred_element_type=jnp.float32)


def beam_power(real_weights, imag_weights, real_volts, imag_volts):
    real_beam = contract(real_weights, real_volts) - contract(imag_weights, imag_volts)
    imag_beam = contract(imag_weights, real_volts) + contract(real_weights, imag_volts)
    return real_beam * real_beam + imag_beam * imag_beam


def per_device(voltages, beam_weights, delay_shifts):
    freq_count = lax.axis_size("freq")
    beam_count = lax.axis_size("beam")
    rows_each = beam_weights.shape[0]
    fourier = fourier_table(F)
    channelized = lax.dot_general(
        fourier, voltages, (((1,), (3,)), ((), ())), preferred_element_type=jnp.float32
    )
    channelized = channelized.astype(jnp.bfloat16).reshape(
        2, F, voltages.shape[0], voltages.shape[2]
    )
    turned = lax.all_to_all(channelized, "freq", split_axis=1, concat_axis=2, tiled=True)
    piece = lax.all_gather(beam_weights, "beam", axis=3, tiled=True)
    powers = beam_power(piece[:, 0], piece[:, 1], turned[0], turned[1])
    grouped = powers.reshape(
        powers.shape[0], beam_count, powers.shape[1] // beam_count, powers.shape[2]
    )
    halved = lax.psum_scatter(
        grouped.astype(jnp.bfloat16), "pol", scatter_dimension=2, tiled=True
    ).astype(jnp.float32)
    regrouped = lax.all_to_all(
        halved.astype(jnp.bfloat16), "beam", split_axis=1, concat_axis=3, tiled=True
    ).astype(halved.dtype)
    summed = regrouped[:, 0]
    planes = summed[:, None]
    local_levels = rows_each.bit_length() - 1
    for level_index in range(local_levels):
        planes = merge_level(planes, delay_shifts[level_index])
    held_rows = planes[0]
    device = lax.axis_index("freq")
    position = jnp.zeros((), jnp.int32)
    half_rows = rows_each // 2
    for section_index in range(freq_count.bit_length() - 1):
        level_now = local_levels + section_index
        high_bit = device // 2**section_index % 2
        lower_side = high_bit == 0
        outgoing = jnp.where(lower_side, held_rows[half_rows:], held_rows[:half_rows])
        received = swapped(outgoing, "freq", section_index)
        first_rows = jnp.where(lower_side, held_rows[:half_rows], received)
        second_rows = jnp.where(lower_side, received, held_rows[half_rows:])
        position = 2 * position + high_bit
        amounts = lax.dynamic_slice_in_dim(delay_shifts[level_now], position * rows_each, rows_each)
        held_rows = jnp.repeat(first_rows, 2, axis=0) + shift_rows(
            jnp.repeat(second_rows, 2, axis=0), amounts
        )
    return (held_rows * (1.0 / (4 * F)))[:, None]


def solution(mesh):
    in_specs = (P("freq", "pol", "beam", None), P("freq", None, None, "beam"), P())
    out_specs = P("freq", "beam", "pol", None)
    return jax.shard_map(
        per_device, mesh=mesh, in_specs=in_specs, out_specs=out_specs, check_vma=False
    )
```

profile of v0, /device:TPU:0, one launch (start us, length us, event | category | flops | bytes accessed | tf_op | source)
XLA Modules:
  0.0 1500.7 jit_solution(10982855420951814088)
XLA Ops:
  6.5 22.9 %copy.25 = bf16[32,2,1024,256]{3,2,0,1:T(8,128)(2,1)} copy(bf16[32,2,1024,256]{3,2,1,0:T(8,128)(2,1)} %param.4) | data formatting | bytes 67108864 | tf_op args[1]
  31.6 24.3 %fusion.6 = bf16[512,128,128]{2,0,1:T(8,128)(2,1)} fusion(bf16[128,1,128,512]{3,2,1,0:T(8,128)(2,1)} %param.3, bf16[256,256]{1,0:T(8,128)(2,1)S(1)} %get-tuple-element.21, bf16[256,256]{1,0:T(8,128)(2,1)S(1)} %get-tuple-element.20, bf16[256,256]{1,0:T(8,128)(2,1)S(1)} %fusion.26), kind=kOutput, calls=%fused_computation.16 | convolution fusion | flops 8600420352 | bytes 33947648 | tf_op jit(solution)/shard_map/dot_general | solution.py:60
  55.9 23.5 %copy.23 = bf16[2,256,128,128]{3,0,2,1:T(2,128)(2,1)S(1)} copy(bf16[2,256,128,128]{3,1,0,2:T(8,128)(2,1)} %bitcast.158) | data formatting | bytes 33554432 | tf_op jit(solution)/shard_map/reshape | solution.py:63
  79.5 370.4 %all_to_all.24 = bf16[2,256,128,128]{3,0,2,1:T(2,128)(2,1)} all-to-all(bf16[2,256,128,128]{3,0,2,1:T(2,128)(2,1)S(1)} %copy.23), channel_id=1, replica_groups=mesh['freq'=8,'pol'=2,'beam'=2] {'freq'}, dimensions={1} | all-to-all | bytes 33554432 | tf_op jit(solution)/shard_map/all_to_all | solution.py:66
  449.9 27.9 %copy.24 = bf16[2,8,32,128,128]{3,1,4,2,0:T(8,128)(2,1)} copy(bf16[2,8,32,128,128]{4,0,3,2,1:T(2,128)(2,1)} %bitcast.152) | data formatting | bytes 33554432 | tf_op jit(solution)/shard_map/all_to_all | solution.py:66
  477.8 11.6 fusion.51
  489.4 13.3 squeeze.10
  502.7 13.3 squeeze.8
  516.0 284.2 %all-gather.2.cloned.1.call-done = bf16[32,2,1024,512]{3,2,0,1:T(8,128)(2,1)} async-done(((bf16[32,2,1024,256]{3,2,0,1:T(8,128)(2,1)}), bf16[32,2,1024,512]{3,2,0,1:T(8,128)(2,1)}) %all-gather.2.cloned.1.call-update) | async-done | bytes 67108880 | tf_op jit(solution)/shard_map/all_gather | solution.py:67
  800.2 19.4 %fusion.1 = f32[32,128,512]{2,1,0:T(8,128)} fusion(bf16[32,1024,128]{1,2,0:T(8,128)(2,1)} %squeeze.8, bf16[32,2,1024,512]{3,2,0,1:T(8,128)(2,1)} %all-gather.2.cloned.1.call-done), kind=kOutput, calls=%fused_computation.11 | convolution fusion | flops 4294967296 | bytes 50331648 | tf_op jit(solution)/shard_map/cab,cas->cbs/dot_general | solution.py:46
  819.6 19.4 %fusion.2 = f32[32,128,512]{2,1,0:T(8,128)} fusion(bf16[32,1024,128]{1,2,0:T(8,128)(2,1)} %squeeze.8, bf16[32,2,1024,512]{3,2,0,1:T(8,128)(2,1)} %all-gather.2.cloned.1.call-done), kind=kOutput, calls=%fused_computation.12 | convolution fusion | flops 4294967296 | bytes 50331648 | tf_op jit(solution)/shard_map/cab,cas->cbs/dot_general | solution.py:46
  839.0 19.4 %fusion = f32[32,128,512]{2,1,0:T(8,128)} fusion(bf16[32,1024,128]{1,2,0:T(8,128)(2,1)} %squeeze.10, bf16[32,2,1024,512]{3,2,0,1:T(8,128)(2,1)} %all-gather.2.cloned.1.call-done), kind=kOutput, calls=%fused_computation.10 | convolution fusion | flops 4294967296 | bytes 50331648 | tf_op jit(solution)/shard_map/cab,cas->cbs/dot_general | solution.py:46
  858.4 25.0 %fusion.9 = bf16[32,512,128]{1,2,0:T(8,128)(2,1)} fusion(f32[32,128,512]{2,1,0:T(8,128)} %fusion.2, f32[32,128,512]{2,1,0:T(8,128)} %fusion, f32[32,128,512]{2,1,0:T(8,128)} %fusion.1, bf16[32,1024,128]{1,2,0:T(8,128)(2,1)} %squeeze.10, bf16[32,2,1024,512]{3,2,0,1:T(8,128)(2,1)} %all-gather.2.cloned.1.call-done), kind=kOutput, calls=%fused_computation.19 | convolution fusion | flops 4307550208 | bytes 71303168 | tf_op jit(solution)/shard_map/cab,cas->cbs/dot_general | solution.py:46
  883.4 6.9 convert_element_type.49
  890.3 14.7 copy.37
  905.0 7.8 reshape.421
  913.5 11.5 reduce-scatter.4.cloned.1.call-done
  925.0 3.4 reshape.422
  928.4 4.0 copy.27
  932.5 3.8 all-to-all-start.1
  936.4 25.4 %all-to-all-done.1 = bf16[32,2,128,128]{2,3,0,1:T(8,128)(2,1)S(1)} async-done(((bf16[32,2,128,128]{2,3,0,1:T(8,128)(2,1)}), bf16[32,2,128,128]{2,3,0,1:T(8,128)(2,1)S(1)}, u32[]{:S(2)}, u32[]{:S(2)}) %all-to-all-start.1) | async-done | bytes 2097184 | tf_op jit(solution)/shard_map/all_to_all | solution.py:75
  965.6 4.2 concatenate.63
  969.8 6.2 gather_fusion
  976.0 4.6 add_bitcast_fusion
  980.6 11.5 slice.144
  992.1 10.0 slice.143
  1004.2 4.2 concatenate.65
  1008.5 6.5 gather_fusion.1
  1015.0 4.5 bitcast_add_fusion.4
  1019.5 21.4 %slice.148 = f32[4,4,128,256]{2,0,3,1:T(4,128)} slice(f32[8,4,128,256]{2,0,3,1:T(8,128)} %bitcast_add_fusion.4), slice={[1:8:2], [0:4:1], [0:128:1], [0:256:1]} | slice | bytes 4194304 | tf_op jit(solution)/shard_map/slice | solution.py:36
  1040.9 19.6 %slice.147 = f32[4,4,128,256]{2,0,3,1:T(4,128)S(1)} slice(f32[8,4,128,256]{2,0,3,1:T(8,128)} %bitcast_add_fusion.4), slice={[0:8:2], [0:4:1], [0:128:1], [0:256:1]} | slice | bytes 4194304 | tf_op jit(solution)/shard_map/slice | solution.py:35
  1063.1 5.4 concatenate.67
  1068.4 9.0 gather_fusion.2
  1077.4 5.1 bitcast_add_fusion.3
  1082.5 39.5 %slice.152 = f32[2,8,128,256]{2,0,3,1:T(2,128)} slice(f32[4,8,128,256]{2,0,3,1:T(4,128)} %bitcast_add_fusion.3), slice={[1:4:2], [0:8:1], [0:128:1], [0:256:1]} | slice | bytes 4194304 | tf_op jit(solution)/shard_map/slice | solution.py:36
  1122.0 36.5 %slice.151 = f32[2,8,128,256]{2,0,3,1:T(2,128)S(1)} slice(f32[4,8,128,256]{2,0,3,1:T(4,128)} %bitcast_add_fusion.3), slice={[0:4:2], [0:8:1], [0:128:1], [0:256:1]} | slice | bytes 4194304 | tf_op jit(solution)/shard_map/slice | solution.py:35
  1160.8 3.3 broadcast_in_dim.69
  1164.1 9.6 concatenate.69
  1173.8 11.9 gather_fusion.3
  1185.6 4.0 bitcast_add_fusion.2
  1189.7 3.2 fusion.52
  1194.1 2.4 broadcast_in_dim.72
  1196.6 4.2 pad_bitcast_fusion
  1200.8 2.6 copy.34
  1203.4 10.3 gather_fusion.4
  1213.8 4.2 broadcast_in_dim.70
  1223.0 45.4 %collective-permute-done = f32[16,128,256]{1,0,2:T(8,128)} collective-permute-done((f32[16,128,256]{1,0,2:T(8,128)S(1)}, f32[16,128,256]{1,0,2:T(8,128)}, u32[]{:S(2)}, u32[]{:S(2)}) %collective-permute-start) | collective-permute-done | bytes 2097184 | tf_op jit(solution)/shard_map/ppermute | solution.py:11
  1268.4 4.7 fusion.13
  1273.2 2.4 broadcast_in_dim.75
  1275.6 4.2 concatenate.73
  1279.9 10.1 gather_fusion.5
  1290.0 4.2 broadcast_in_dim.74
  1299.6 44.7 %collective-permute-done.1 = f32[16,128,256]{1,0,2:T(8,128)} collective-permute-done((f32[16,128,256]{1,0,2:T(8,128)S(1)}, f32[16,128,256]{1,0,2:T(8,128)}, u32[]{:S(2)}, u32[]{:S(2)}) %collective-permute-start.1) | collective-permute-done | bytes 2097184 | tf_op jit(solution)/shard_map/ppermute | solution.py:11
  1344.2 4.7 slice_select_fusion.3
  1351.4 4.2 concatenate.75
  1355.6 10.1 gather_fusion.6
  1365.7 4.2 broadcast_in_dim.76
  1373.6 88.9 %collective-permute-done.2 = f32[16,128,256]{1,0,2:T(8,128)S(1)} collective-permute-done((f32[16,128,256]{1,0,2:T(8,128)S(1)}, f32[16,128,256]{1,0,2:T(8,128)S(1)}, u32[]{:S(2)}, u32[]{:S(2)}) %collective-permute-start.2) | collective-permute-done | bytes 2097184 | tf_op jit(solution)/shard_map/ppermute | solution.py:11
  1464.3 2.6 broadcast_in_dim.79
  1466.9 4.2 concatenate.77
  1471.1 10.1 gather_fusion.7
  1481.2 4.2 broadcast_in_dim.78
  1485.4 3.0 fusion.10
  1488.4 5.2 copy.36
  (49 shorter events, 33.2 us)
Async XLA Ops:
  6.5 793.7 %all-gather.2.cloned.1.call-start = ((), (), s32[]{:S(2)}) async-start(), calls=%async_computation.3 | async-start | bytes 100663296 | tf_op jit(solution)/shard_map/all_gather | solution.py:67
  29.4 895.6 %reduce-scatter.4.cloned.1.call-start = ((), (), s32[]{:S(2)}) async-start(), calls=%async_computation.4 | async-start | bytes 6291456
  912.8 0.7 copy-start.6
  932.5 29.3 %all-to-all-start.1 = ((bf16[32,2,128,128]{2,3,0,1:T(8,128)(2,1)}), bf16[32,2,128,128]{2,3,0,1:T(8,128)(2,1)S(1)}, u32[]{:S(2)}, u32[]{:S(2)}) async-start(bf16[32,2,128,128]{2,3,0,1:T(8,128)(2,1)} %copy.27), calls=%async_computation.1 | async-start | bytes 4194304 | tf_op jit(solution)/shard_map/all_to_all | solution.py:75
  1213.8 4.2 copy-start.5
  1219.0 2.0 copy-start.1
  1221.3 47.2 %collective-permute-start = (f32[16,128,256]{1,0,2:T(8,128)S(1)}, f32[16,128,256]{1,0,2:T(8,128)}, u32[]{:S(2)}, u32[]{:S(2)}) collective-permute-start(f32[16,128,256]{1,0,2:T(8,128)S(1)} %fusion.12), channel_id=1, source_target_pairs={{0,4},{4,0},{8,12},{12,8},{16,20},{20,16},{24,28},{28,24},{1,5},{5... | collective-permute-start | bytes 6291464 | tf_op jit(solution)/shard_map/ppermute | solution.py:11
  1290.0 4.2 copy-start.2
  1295.6 2.0 copy-start
  1297.9 46.3 %collective-permute-start.1 = (f32[16,128,256]{1,0,2:T(8,128)S(1)}, f32[16,128,256]{1,0,2:T(8,128)}, u32[]{:S(2)}, u32[]{:S(2)}) collective-permute-start(f32[16,128,256]{1,0,2:T(8,128)S(1)} %slice_select_fusion.4), channel_id=1, source_target_pairs={{0,8},{4,12},{8,0},{12,4},{16,24},{20,28},{24,16},{28,20},{1,9},{5... | collective-permute-start | bytes 6291464 | tf_op jit(solution)/shard_map/ppermute | solution.py:11
  1365.7 4.2 copy-start.3
  1371.3 91.2 %collective-permute-start.2 = (f32[16,128,256]{1,0,2:T(8,128)S(1)}, f32[16,128,256]{1,0,2:T(8,128)S(1)}, u32[]{:S(2)}, u32[]{:S(2)}) collective-permute-start(f32[16,128,256]{1,0,2:T(8,128)S(1)} %slice_select_fusion.1), channel_id=1, source_target_pairs={{0,16},{4,20},{8,24},{12,28},{16,0},{20,4},{24,8},{28,12},{1,17},{... | collective-permute-start | bytes 6291464 | tf_op jit(solution)/shard_map/ppermute | solution.py:11
  1481.2 4.2 copy-start.4
Sparse Core Ops, SparseCore 0:
  29.5 770.6 all-gather.1
  912.9 12.0 reduce-scatter.3
where the time goes:
time: 1520 us; the launch traced here: 1500 us
  waiting for transfers between devices  500 us (33%)
  local copies, waits for them, and re-layouts  460 us (30%)
  blocking collectives  370 us (24%)
  matrix products  108 us (7%)
  other arithmetic  39.6 us (3%)
    all_to_all x1, blocking collectives, per_device(): lax.all_to_all(channelized, 'freq', split_axis=1, concat_axis=2, tiled=True)  370 us
    all_gather x1, waiting for transfers between devices, per_device(): piece = lax.all_gather(beam_weights, 'beam', axis=3, tiled=True)  284 us
    ppermute x3, waiting for transfers between devices, swapped(): lax.ppermute(shard, axis, [(i, i ^ 1 << bit) for i in range(lax.axis_size...  179 us
    slice x9, local copies, waits for them, and re-layouts, merge_level(): second_half = planes[1::2]  84 us
    dot_general x4, matrix products, contract(): jnp.einsum('cab,cas->cbs', weights_part, volts_part, preferred_element_ty...  83.2 us
    gather x8, local copies, waits for them, and re-layouts, shift_rows(): lax.dynamic_slice_in_dim(single_plane, amount, length, axis=1)  74.2 us
    slice x6, local copies, waits for them, and re-layouts, merge_level(): first_half = planes[0::2]  70.3 us
    unnamed x18, local copies, waits for them, and re-layouts  53.4 us
  transfers between devices with their start and end apart: 6, of which 6 were waited for; matrix products, arithmetic and copies ran while one was open for 8% of the time, Pallas kernels for 0%

commit v1 on v0

--- a/solution.py
+++ b/solution.py
@@ -63,7 +63,21 @@
     channelized = channelized.astype(jnp.bfloat16).reshape(
         2, F, voltages.shape[0], voltages.shape[2]
     )
-    turned = lax.all_to_all(channelized, "freq", split_axis=1, concat_axis=2, tiled=True)
+    now = jax.lax.psum(1, "freq")
+    carry_in = jax.lax.axis_index("freq")
+    shaped, arr_out = (now, carry_in)
+    val = channelized.shape[1] // shaped
+    piece_next = jnp.roll(channelized, shift=-arr_out * val, axis=1)
+    by_rank = [lax.slice_in_dim(piece_next, 0, val, axis=1)]
+    for k in range(1, shaped):
+        current_block = lax.slice_in_dim(piece_next, k * val, (k + 1) * val, axis=1)
+        k_now = jax.lax.ppermute(
+            current_block, "freq", [(b, (b + k) % shaped) for b in range(shaped)]
+        )
+        by_rank.append(k_now)
+    turned = jnp.roll(
+        jnp.concatenate(by_rank[::-1], axis=2), (arr_out + 1) * by_rank[0].shape[2], axis=2
+    )
     piece = lax.all_gather(beam_weights, "beam", axis=3, tiled=True)
     powers = beam_power(piece[:, 0], piece[:, 1], turned[0], turned[1])
     grouped = powers.reshape(

time: 1520 us -> 1520 us (level)
  blocking collectives: 370 us -> 0 us
  waiting for transfers between devices: 500 us -> 856 us
    all_to_all x1 -> x0, blocking collectives: 370 us -> none  [per_device(): lax.all_to_all(channelized, 'freq', split_axis=1, concat_axis=2, tiled=True)]
    ppermute x0 -> x7, waiting for transfers between devices: none -> 347 us  [per_device(): jax.lax.ppermute(current_block, 'freq', [(b, (b + k) % shaped) for b in r...]
    unnamed x18 -> x35, local copies, waits for them, and re-layouts: 53.4 us -> 102 us
    all_to_all x1 -> x0, local copies, waits for them, and re-layouts: 27.9 us -> none  [per_device(): lax.all_to_all(channelized, 'freq', split_axis=1, concat_axis=2, tiled=True)]
    squeeze x2 -> x0, local copies, waits for them, and re-layouts: 26.6 us -> none  [per_device(): powers = beam_power(piece[:, 0], piece[:, 1], turned[0], turned[1])]
  transfers between devices with their start and end apart: 6 -> 13, of which waited for: 6 -> 10; matrix products, arithmetic and copies ran while one was open for 8% -> 8% of each run, Pallas kernels for 0% -> 0%
where the time goes in v1:
time: 1520 us; the launch traced here: 1500 us
  waiting for transfers between devices  856 us (56%)
  local copies, waits for them, and re-layouts  454 us (30%)
  matrix products  107 us (7%)
  other arithmetic  50.4 us (3%)
  starting transfers between devices  19.5 us (1%)
    ppermute x7, waiting for transfers between devices, per_device(): jax.lax.ppermute(current_block, 'freq', [(b, (b + k) % shaped) for b in r...  347 us
    all_gather x1, waiting for transfers between devices, per_device(): piece = lax.all_gather(beam_weights, 'beam', axis=3, tiled=True)  293 us
    ppermute x3, waiting for transfers between devices, swapped(): lax.ppermute(shard, axis, [(i, i ^ 1 << bit) for i in range(lax.axis_size...  179 us
    unnamed x35, local copies, waits for them, and re-layouts  102 us
    slice x9, local copies, waits for them, and re-layouts, merge_level(): second_half = planes[1::2]  84.1 us
    dot_general x4, matrix products, contract(): jnp.einsum('cab,cas->cbs', weights_part, volts_part, preferred_element_ty...  82.2 us
    gather x8, local copies, waits for them, and re-layouts, shift_rows(): lax.dynamic_slice_in_dim(single_plane, amount, length, axis=1)  74.2 us
    slice x6, local copies, waits for them, and re-layouts, merge_level(): first_half = planes[0::2]  70.3 us
  transfers between devices with their start and end apart: 13, of which 10 were waited for; matrix products, arithmetic and copies ran while one was open for 8% of the time, Pallas kernels for 0%

profile of v1, /device:TPU:0, one launch (start us, length us, event | category | flops | bytes accessed | tf_op | source)
XLA Modules:
  0.0 1499.7 jit_solution(10004434868820856724)
XLA Ops:
  6.5 22.9 %copy.27 = bf16[32,2,1024,256]{3,2,0,1:T(8,128)(2,1)} copy(bf16[32,2,1024,256]{3,2,1,0:T(8,128)(2,1)} %param.4) | data formatting | bytes 67108864 | tf_op args[1]
  31.6 24.4 %fusion.7 = bf16[512,128,128]{2,0,1:T(8,128)(2,1)} fusion(bf16[128,1,128,512]{3,2,1,0:T(8,128)(2,1)} %param.3, bf16[256,256]{1,0:T(8,128)(2,1)S(1)} %get-tuple-element.30, bf16[256,256]{1,0:T(8,128)(2,1)S(1)} %get-tuple-element.29, bf16[256,256]{1,0:T(8,128)(2,1)S(1)} %fusion.27), kind=kOutput, calls=%fused_computation.19 | convolution fusion | flops 8600420352 | bytes 33947648 | tf_op jit(solution)/shard_map/dot_general | solution.py:60
  56.0 25.4 %copy.25 = bf16[2,256,128,128]{2,3,1,0:T(8,128)(2,1)} copy(bf16[2,256,128,128]{3,1,0,2:T(8,128)(2,1)} %bitcast.152) | data formatting | bytes 33554432 | tf_op jit(solution)/shard_map/reshape | solution.py:63
  81.4 11.0 fusion.4
  92.4 5.7 fusion.56
  98.1 3.5 copy-done
  101.6 6.2 collective-permute-start
  111.3 42.6 %collective-permute-done = bf16[2,32,128,128]{2,3,1,0:T(8,128)(2,1)S(1)} collective-permute-done((bf16[2,32,128,128]{2,3,1,0:T(8,128)(2,1)S(1)}, bf16[2,32,128,128]{2,3,1,0:T(8,128)(2,1)S(1)}, u32[]{:S(2)}, u32[]{:S(2)}) %collective-permute-start) | collective-permute-done | bytes 2097184 | tf_op jit(solution)/shard_map/ppermute | solution.py:74
  153.9 44.9 %collective-permute-done.1 = bf16[2,32,128,128]{2,3,1,0:T(8,128)(2,1)} collective-permute-done((bf16[2,32,128,128]{2,3,1,0:T(8,128)(2,1)S(1)}, bf16[2,32,128,128]{2,3,1,0:T(8,128)(2,1)}, u32[]{:S(2)}, u32[]{:S(2)}) %collective-permute-start.1) | collective-permute-done | bytes 2097184 | tf_op jit(solution)/shard_map/ppermute | solution.py:74
  200.4 3.3 constant_dynamic-update-slice_fusion.12
  203.7 40.2 %collective-permute-done.2 = bf16[2,32,128,128]{2,3,1,0:T(8,128)(2,1)} collective-permute-done((bf16[2,32,128,128]{2,3,1,0:T(8,128)(2,1)}, bf16[2,32,128,128]{2,3,1,0:T(8,128)(2,1)}, u32[]{:S(2)}, u32[]{:S(2)}) %collective-permute-start.2) | collective-permute-done | bytes 2097184 | tf_op jit(solution)/shard_map/ppermute | solution.py:74
  243.9 3.3 constant_dynamic-update-slice_fusion.11
  247.3 219.6 %collective-permute-done.3 = bf16[2,32,128,128]{2,3,1,0:T(8,128)(2,1)} collective-permute-done((bf16[2,32,128,128]{2,3,1,0:T(8,128)(2,1)}, bf16[2,32,128,128]{2,3,1,0:T(8,128)(2,1)}, u32[]{:S(2)}, u32[]{:S(2)}) %collective-permute-start.3) | collective-permute-done | bytes 2097184 | tf_op jit(solution)/shard_map/ppermute | solution.py:74
  494.4 3.3 constant_dynamic-update-slice_fusion.2
  497.7 3.3 constant_dynamic-update-slice_fusion.1
  507.6 292.6 %all-gather.2.cloned.1.call-done = bf16[32,2,1024,512]{3,2,0,1:T(8,128)(2,1)} async-done(((bf16[32,2,1024,256]{3,2,0,1:T(8,128)(2,1)}), bf16[32,2,1024,512]{3,2,0,1:T(8,128)(2,1)}) %all-gather.2.cloned.1.call-update) | async-done | bytes 67108880 | tf_op jit(solution)/shard_map/all_gather | solution.py:81
  800.2 19.6 %fusion.1 = f32[32,128,512]{2,1,0:T(8,128)} fusion(bf16[32,2,1024,512]{3,2,0,1:T(8,128)(2,1)} %all-gather.2.cloned.1.call-done, bf16[2,32,2048,128]{2,3,1,0:T(8,128)(2,1)} %slice_dynamic-update-slice_fusion.1, s32[]{:T(128)S(6)} %select_n.202), kind=kOutput, calls=%fused_computation.13 | convolution fusion | flops 4294967296 | bytes 50331652 | tf_op jit(solution)/shard_map/cab,cas->cbs/dot_general | solution.py:46
  819.8 19.4 %fusion.3 = f32[32,128,512]{2,1,0:T(8,128)} fusion(bf16[32,2,1024,512]{3,2,0,1:T(8,128)(2,1)} %all-gather.2.cloned.1.call-done, bf16[2,32,2048,128]{2,3,1,0:T(8,128)(2,1)} %slice_dynamic-update-slice_fusion.1, s32[]{:T(128)S(6)} %add.256, s32[]{:T(128)S(6)} %select_n.202), kind=kOutput, calls=%fused_computation.15 | convolution fusion | flops 4294967296 | bytes 50331656 | tf_op jit(solution)/shard_map/cab,cas->cbs/dot_general | solution.py:46
  839.2 19.4 %fusion = f32[32,128,512]{2,1,0:T(8,128)} fusion(bf16[32,2,1024,512]{3,2,0,1:T(8,128)(2,1)} %all-gather.2.cloned.1.call-done, bf16[2,32,2048,128]{2,3,1,0:T(8,128)(2,1)} %slice_dynamic-update-slice_fusion.1, s32[]{:T(128)S(6)} %add.256, s32[]{:T(128)S(6)} %select_n.202), kind=kOutput, calls=%fused_computation.12 | convolution fusion | flops 4294967296 | bytes 50331656 | tf_op jit(solution)/shard_map/cab,cas->cbs/dot_general | solution.py:46
  858.6 23.9 %fusion.10 = bf16[32,512,128]{1,2,0:T(8,128)(2,1)} fusion(f32[32,128,512]{2,1,0:T(8,128)} %fusion, f32[32,128,512]{2,1,0:T(8,128)} %fusion.1, f32[32,128,512]{2,1,0:T(8,128)} %fusion.3, bf16[32,2,1024,512]{3,2,0,1:T(8,128)(2,1)} %all-gather.2.cloned.1.call-done, bf16[2,32,2048,128]{2,3,1,0:T(8,128)(2,1)} %slice_dynamic-update-slice_fusion.1, s32[]{:T(128)S(6)} %select_n.202), kind=kOutput, calls=%fused_computation.24 | convolution fusion | flops 4307550208 | bytes 71303168 | tf_op jit(solution)/shard_map/cab,cas->cbs/dot_general | solution.py:46
  882.5 6.9 convert_element_type.49
  889.4 14.7 copy.39
  904.0 7.8 reshape.417
  912.5 11.5 reduce-scatter.4.cloned.1.call-done
  927.3 4.0 copy.29
  931.3 4.0 all-to-all-start
  935.5 25.4 %all-to-all-done = bf16[32,2,128,128]{2,3,0,1:T(8,128)(2,1)S(1)} async-done(((bf16[32,2,128,128]{2,3,0,1:T(8,128)(2,1)}), bf16[32,2,128,128]{2,3,0,1:T(8,128)(2,1)S(1)}, u32[]{:S(2)}, u32[]{:S(2)}) %all-to-all-start) | async-done | bytes 2097184 | tf_op jit(solution)/shard_map/all_to_all | solution.py:89
  964.6 4.2 concatenate.75
  968.9 6.2 gather_fusion
  975.1 4.6 add_bitcast_fusion
  979.7 11.6 slice.174
  991.2 10.0 slice.173
  1003.3 4.2 concatenate.77
  1007.6 6.5 gather_fusion.1
  1014.1 4.5 bitcast_add_fusion.4
  1018.6 21.3 %slice.178 = f32[4,4,128,256]{2,0,3,1:T(4,128)} slice(f32[8,4,128,256]{2,0,3,1:T(8,128)} %bitcast_add_fusion.4), slice={[1:8:2], [0:4:1], [0:128:1], [0:256:1]} | slice | bytes 4194304 | tf_op jit(solution)/shard_map/slice | solution.py:36
  1040.0 19.6 %slice.177 = f32[4,4,128,256]{2,0,3,1:T(4,128)S(1)} slice(f32[8,4,128,256]{2,0,3,1:T(8,128)} %bitcast_add_fusion.4), slice={[0:8:2], [0:4:1], [0:128:1], [0:256:1]} | slice | bytes 4194304 | tf_op jit(solution)/shard_map/slice | solution.py:35
  1062.2 5.4 concatenate.79
  1067.6 9.0 gather_fusion.2
  1076.5 5.1 bitcast_add_fusion.3
  1081.6 39.5 %slice.182 = f32[2,8,128,256]{2,0,3,1:T(2,128)} slice(f32[4,8,128,256]{2,0,3,1:T(4,128)} %bitcast_add_fusion.3), slice={[1:4:2], [0:8:1], [0:128:1], [0:256:1]} | slice | bytes 4194304 | tf_op jit(solution)/shard_map/slice | solution.py:36
  1121.1 36.5 %slice.181 = f32[2,8,128,256]{2,0,3,1:T(2,128)S(1)} slice(f32[4,8,128,256]{2,0,3,1:T(4,128)} %bitcast_add_fusion.3), slice={[0:4:2], [0:8:1], [0:128:1], [0:256:1]} | slice | bytes 4194304 | tf_op jit(solution)/shard_map/slice | solution.py:35
  1159.9 3.3 broadcast_in_dim.69
  1163.3 9.6 concatenate.81
  1172.9 11.9 gather_fusion.3
  1184.8 4.0 bitcast_add_fusion.2
  1195.7 4.3 pad_bitcast_fusion
  1202.6 10.3 gather_fusion.4
  1212.9 4.2 broadcast_in_dim.70
  1222.2 45.4 %collective-permute-done.7 = f32[16,128,256]{1,0,2:T(8,128)} collective-permute-done((f32[16,128,256]{1,0,2:T(8,128)S(1)}, f32[16,128,256]{1,0,2:T(8,128)}, u32[]{:S(2)}, u32[]{:S(2)}) %collective-permute-start.7) | collective-permute-done | bytes 2097184 | tf_op jit(solution)/shard_map/ppermute | solution.py:11
  1267.6 4.7 fusion.14
  1274.7 4.3 concatenate.85
  1279.0 10.1 gather_fusion.5
  1289.1 4.2 broadcast_in_dim.74
  1298.7 44.6 %collective-permute-done.8 = f32[16,128,256]{1,0,2:T(8,128)} collective-permute-done((f32[16,128,256]{1,0,2:T(8,128)S(1)}, f32[16,128,256]{1,0,2:T(8,128)}, u32[]{:S(2)}, u32[]{:S(2)}) %collective-permute-start.8) | collective-permute-done | bytes 2097184 | tf_op jit(solution)/shard_map/ppermute | solution.py:11
  1343.3 4.7 slice_select_fusion.3
  1350.4 4.3 concatenate.87
  1354.7 10.1 gather_fusion.6
  1364.8 4.2 broadcast_in_dim.76
  1372.7 88.8 %collective-permute-done.9 = f32[16,128,256]{1,0,2:T(8,128)S(1)} collective-permute-done((f32[16,128,256]{1,0,2:T(8,128)S(1)}, f32[16,128,256]{1,0,2:T(8,128)S(1)}, u32[]{:S(2)}, u32[]{:S(2)}) %collective-permute-start.9) | collective-permute-done | bytes 2097184 | tf_op jit(solution)/shard_map/ppermute | solution.py:11
  1465.9 4.3 concatenate.89
  1470.1 10.1 gather_fusion.7
  1480.3 4.2 broadcast_in_dim.78
  1487.5 5.2 copy.38
  (78 shorter events, 92.0 us)
Async XLA Ops:
  6.5 793.7 %all-gather.2.cloned.1.call-start = ((), (), s32[]{:S(2)}) async-start(), calls=%async_computation.2 | async-start | bytes 100663296 | tf_op jit(solution)/shard_map/all_gather | solution.py:81
  29.4 894.6 %reduce-scatter.4.cloned.1.call-start = ((), (), s32[]{:S(2)}) async-start(), calls=%async_computation.3 | async-start | bytes 6291456
  92.4 9.3 copy-start
  101.6 52.3 %collective-permute-start = (bf16[2,32,128,128]{2,3,1,0:T(8,128)(2,1)S(1)}, bf16[2,32,128,128]{2,3,1,0:T(8,128)(2,1)S(1)}, u32[]{:S(2)}, u32[]{:S(2)}) collective-permute-start(bf16[2,32,128,128]{2,3,1,0:T(8,128)(2,1)S(1)} %get-tuple-element.11), channel_id=1, source_target_pairs={{0,28},{4,0},{8,4},{12,8},{16,12},{20,16},{24,20},{28,24},{1,29},{... | collective-permute-start | bytes 6291464 | tf_op jit(solution)/shard_map/ppermute | solution.py:74
  107.8 91.0 %collective-permute-start.1 = (bf16[2,32,128,128]{2,3,1,0:T(8,128)(2,1)S(1)}, bf16[2,32,128,128]{2,3,1,0:T(8,128)(2,1)}, u32[]{:S(2)}, u32[]{:S(2)}) collective-permute-start(bf16[2,32,128,128]{2,3,1,0:T(8,128)(2,1)S(1)} %get-tuple-element.10), channel_id=1, source_target_pairs={{0,24},{4,28},{8,0},{12,4},{16,8},{20,12},{24,16},{28,20},{1,25},{... | collective-permute-start | bytes 6291464 | tf_op jit(solution)/shard_map/ppermute | solution.py:74
  108.3 135.7 %collective-permute-start.2 = (bf16[2,32,128,128]{2,3,1,0:T(8,128)(2,1)}, bf16[2,32,128,128]{2,3,1,0:T(8,128)(2,1)}, u32[]{:S(2)}, u32[]{:S(2)}) collective-permute-start(bf16[2,32,128,128]{2,3,1,0:T(8,128)(2,1)} %get-tuple-element.9), channel_id=1, source_target_pairs={{0,20},{4,24},{8,28},{12,0},{16,4},{20,8},{24,12},{28,16},{1,21},{... | collective-permute-start | bytes 6291464 | tf_op jit(solution)/shard_map/ppermute | solution.py:74
  108.3 358.5 %collective-permute-start.3 = (bf16[2,32,128,128]{2,3,1,0:T(8,128)(2,1)}, bf16[2,32,128,128]{2,3,1,0:T(8,128)(2,1)}, u32[]{:S(2)}, u32[]{:S(2)}) collective-permute-start(bf16[2,32,128,128]{2,3,1,0:T(8,128)(2,1)} %get-tuple-element.8), channel_id=1, source_target_pairs={{0,16},{4,20},{8,24},{12,28},{16,0},{20,4},{24,8},{28,12},{1,17},{... | collective-permute-start | bytes 6291464 | tf_op jit(solution)/shard_map/ppermute | solution.py:74
  111.3 358.7 %collective-permute-start.4 = (bf16[2,32,128,128]{2,3,1,0:T(8,128)(2,1)}, bf16[2,32,128,128]{2,3,1,0:T(8,128)(2,1)}, u32[]{:S(2)}, u32[]{:S(2)}) collective-permute-start(bf16[2,32,128,128]{2,3,1,0:T(8,128)(2,1)} %get-tuple-element.7), channel_id=1, source_target_pairs={{0,12},{4,16},{8,20},{12,24},{16,28},{20,0},{24,4},{28,8},{1,13},{... | collective-permute-start | bytes 6291464 | tf_op jit(solution)/shard_map/ppermute | solution.py:74
  153.9 319.4 %collective-permute-start.5 = (bf16[2,32,128,128]{2,3,1,0:T(8,128)(2,1)}, bf16[2,32,128,128]{2,3,1,0:T(8,128)(2,1)}, u32[]{:S(2)}, u32[]{:S(2)}) collective-permute-start(bf16[2,32,128,128]{2,3,1,0:T(8,128)(2,1)} %get-tuple-element.6), channel_id=1, source_target_pairs={{0,8},{4,12},{8,16},{12,20},{16,24},{20,28},{24,0},{28,4},{1,9},{5... | collective-permute-start | bytes 6291464 | tf_op jit(solution)/shard_map/ppermute | solution.py:74
  198.9 277.8 %collective-permute-start.6 = (bf16[2,32,128,128]{2,3,1,0:T(8,128)(2,1)}, bf16[2,32,128,128]{2,3,1,0:T(8,128)(2,1)}, u32[]{:S(2)}, u32[]{:S(2)}) collective-permute-start(bf16[2,32,128,128]{2,3,1,0:T(8,128)(2,1)} %get-tuple-element.5), channel_id=1, source_target_pairs={{0,4},{4,8},{8,12},{12,16},{16,20},{20,24},{24,28},{28,0},{1,5},{5... | collective-permute-start | bytes 6291464 | tf_op jit(solution)/shard_map/ppermute | solution.py:74
  911.8 0.7 copy-start.7
  931.3 29.5 %all-to-all-start = ((bf16[32,2,128,128]{2,3,0,1:T(8,128)(2,1)}), bf16[32,2,128,128]{2,3,0,1:T(8,128)(2,1)S(1)}, u32[]{:S(2)}, u32[]{:S(2)}) async-start(bf16[32,2,128,128]{2,3,0,1:T(8,128)(2,1)} %copy.29), calls=%async_computation | async-start | bytes 4194304 | tf_op jit(solution)/shard_map/all_to_all | solution.py:89
  1212.9 4.2 copy-start.6
  1218.1 2.0 copy-start.2
  1220.4 47.2 %collective-permute-start.7 = (f32[16,128,256]{1,0,2:T(8,128)S(1)}, f32[16,128,256]{1,0,2:T(8,128)}, u32[]{:S(2)}, u32[]{:S(2)}) collective-permute-start(f32[16,128,256]{1,0,2:T(8,128)S(1)} %fusion.13), channel_id=1, source_target_pairs={{0,4},{4,0},{8,12},{12,8},{16,20},{20,16},{24,28},{28,24},{1,5},{5... | collective-permute-start | bytes 6291464 | tf_op jit(solution)/shard_map/ppermute | solution.py:11
  1289.1 4.2 copy-start.3
  1294.7 2.0 copy-start.1
  1297.0 46.3 %collective-permute-start.8 = (f32[16,128,256]{1,0,2:T(8,128)S(1)}, f32[16,128,256]{1,0,2:T(8,128)}, u32[]{:S(2)}, u32[]{:S(2)}) collective-permute-start(f32[16,128,256]{1,0,2:T(8,128)S(1)} %slice_select_fusion.4), channel_id=1, source_target_pairs={{0,8},{4,12},{8,0},{12,4},{16,24},{20,28},{24,16},{28,20},{1,9},{5... | collective-permute-start | bytes 6291464 | tf_op jit(solution)/shard_map/ppermute | solution.py:11
  1364.8 4.2 copy-start.4
  1370.3 91.2 %collective-permute-start.9 = (f32[16,128,256]{1,0,2:T(8,128)S(1)}, f32[16,128,256]{1,0,2:T(8,128)S(1)}, u32[]{:S(2)}, u32[]{:S(2)}) collective-permute-start(f32[16,128,256]{1,0,2:T(8,128)S(1)} %slice_select_fusion.1), channel_id=1, source_target_pairs={{0,16},{4,20},{8,24},{12,28},{16,0},{20,4},{24,8},{28,12},{1,17},{... | collective-permute-start | bytes 6291464 | tf_op jit(solution)/shard_map/ppermute | solution.py:11
  1480.3 4.2 copy-start.5
Sparse Core Ops, SparseCore 0:
  29.6 770.6 all-gather.1
  912.0 12.0 reduce-scatter.3
